TPU v7x, 32 devices: a whole 2x2x4 slice. The times are simulated.
32 devices in a mesh: ia: 4 (over y, core), ja: 2 (over x), ka: 4 (over z).
Axes of the slice: x: 2, y: 2, z: 4, core: 2. Of those that a mesh axis runs over, the one named last changes fastest.
Arguments:
- block_coords: int32 [4, 2, 4, 4, 3], P('ia', 'ja', 'ka'), may hold values from 0 to 3, as said below
- live_blocks: int32 [4, 2, 4], P('ia', 'ja', 'ka'), may hold values from 1 to 4, as said below
- counts: int32 [4, 2, 4, 4, 64, 4096], P('ia', 'ja', 'ka'), may hold values from 0 to 7
- factor_a: float32 [1024, 256], P(('ia', 'ja', 'ka')), may hold values from 0.3 to 9.6
- factor_b: float32 [512, 256], P(('ja', 'ka')), may hold values from 0.05 to 8
- factor_c: float32 [1024, 256], P('ka', 'ia'), may hold values from 0.05 to 8
Outputs:
- factor_new: float32 [1024, 256], P(('ia', 'ja', 'ka'))
Inputs may be any that keep to these rules, and one draw needn't show every extreme that they name: `block_coords`: a device's slots name distinct blocks; slot 0 is always live, and every mode-1 block of the slab has a live block on some device. `live_blocks`: on some device all 4 slots are live.
All inputs are finite; a program needn't handle non-finite values.
Results may differ from a plain program's by a relative error of at most 0.00061.
Values may be sent and summed in bfloat16 or wider, within the bound.
A program may use at most 64 MiB of HBM per device.

v0:
```python
import jax
import jax.numpy as jnp
from jax import lax
from jax.sharding import PartitionSpec as P

R = 256
BS = 64
RB1 = 4
RB2 = 4
RB3 = 4
SLOTS = 4


def make_panel(rows_b, rows_c, index_j, index_k):
    piece_b = lax.dynamic_slice_in_dim(rows_b, index_j * BS, BS, 0)
    piece_c = lax.dynamic_slice_in_dim(rows_c, index_k * BS, BS, 0)
    return (piece_b[:, None, :] * piece_c[None, :, :]).reshape(BS * BS, R).astype(jnp.bfloat16)


def add_block(phi, factor_low, panel, index_i, weight, block_counts):
    block_a = lax.dynamic_slice_in_dim(factor_low, index_i * BS, BS, 0)
    model = lax.dot_general(
        block_a, panel, (((1,), (1,)), ((), ())), preferred_element_type=jnp.float32
    )
    ratio = (block_counts.astype(jnp.float32) / model).astype(jnp.bfloat16)
    part = jnp.dot(ratio, panel, preferred_element_type=jnp.float32) * weight
    old = lax.dynamic_slice_in_dim(phi, index_i * BS, BS, 0)
    return lax.dynamic_update_slice_in_dim(phi, old + part, index_i * BS, 0)


def local(block_coords, live_blocks, counts, factor_a, factor_b, factor_c):
    coords = block_coords.reshape(SLOTS, 3)
    local_counts = counts.reshape(SLOTS, BS, BS * BS)
    weights = (jnp.arange(SLOTS, dtype=jnp.int32) < live_blocks.reshape(())).astype(jnp.float32)
    rows_b = lax.all_gather(factor_b, "ka", axis=0, tiled=True)
    rows_c = lax.all_gather(factor_c, "ia", axis=1, tiled=True)
    sums_b = rows_b.reshape(RB2, BS, R).sum(axis=1)
    sums_c = rows_c.reshape(RB3, BS, R).sum(axis=1)
    pick_j = (coords[:, 1:2] == jnp.arange(RB2, dtype=jnp.int32)[None, :]).astype(jnp.float32)
    pick_k = (coords[:, 2:3] == jnp.arange(RB3, dtype=jnp.int32)[None, :]).astype(jnp.float32)
    masses = jnp.dot(pick_j, sums_b, precision=lax.Precision.HIGHEST) * jnp.dot(
        pick_k, sums_c, precision=lax.Precision.HIGHEST
    )
    pick_i = (coords[:, 0:1] == jnp.arange(RB1, dtype=jnp.int32)[None, :]).astype(
        jnp.float32
    ) * weights[:, None]
    mass_part = lax.dot_general(
        pick_i, masses, (((0,), (0,)), ((), ())), precision=lax.Precision.HIGHEST
    )
    mass = lax.psum(mass_part, ("ja", "ka"))
    mass_rows = jnp.broadcast_to(mass[:, None, :], (RB1, BS, R)).reshape(RB1 * BS, R)
    owned = factor_a.shape[0]
    first_row = lax.axis_index(("ja", "ka")) * owned
    my_mass = lax.dynamic_slice_in_dim(mass_rows, first_row, owned, 0)
    empty = jnp.zeros((RB1 * BS, R), jnp.float32)

    def accumulate(factor_low):

        def step(phi, item):
            index_i, index_j, index_k, weight, block_counts = item
            panel = make_panel(rows_b, rows_c, index_j, index_k)
            return (add_block(phi, factor_low, panel, index_i, weight, block_counts), None)

        phi, _ = lax.scan(
            step, empty, (coords[:, 0], coords[:, 1], coords[:, 2], weights, local_counts)
        )
        return phi

    whole = lax.all_gather(factor_a, ("ja", "ka"), axis=0, tiled=True)
    phi = accumulate(whole.astype(jnp.bfloat16))
    totals = lax.psum(phi, ("ja", "ka"))
    updated = whole * totals / mass_rows
    phi = accumulate(updated.astype(jnp.bfloat16))
    mine = lax.psum_scatter(phi, ("ja", "ka"), scatter_dimension=0, tiled=True)
    return lax.dynamic_slice_in_dim(updated, first_row, owned, 0) * mine / my_mass


def solution(mesh):
    placed = (
        P("ia", "ja", "ka", None, None),
        P("ia", "ja", "ka"),
        P("ia", "ja", "ka", None, None, None),
        P(("ia", "ja", "ka"), None),
        P(("ja", "ka"), None),
        P("ka", "ia"),
    )
    return jax.shard_map(
        local, mesh=mesh, in_specs=placed, out_specs=P(("ia", "ja", "ka"), None), check_vma=False
    )
```

profile of v0, /device:TPU:0, one launch (start us, length us, event | category | flops | bytes accessed | tf_op | source)
XLA Modules:
  0.0 275.6 jit_solution(7233616077265290646)
XLA Ops:
  6.5 0.8 copy.14
  7.5 7.5 %all_gather.11 = f32[256,256]{0,1:T(8,128)S(1)} all-gather(f32[256,64]{0,1:T(8,128)} %param.15), channel_id=1, replica_groups=mesh['ia'=4,'ja'=2,'ka'=4] {'ia'}, dimensions={1}, use_global_device_ids=true | all-gather | bytes 327680 | tf_op jit(solution)/shard_map/all_gather | solution.py:36
  15.1 14.3 %all_gather.10 = f32[256,256]{1,0:T(8,128)S(1)} all-gather(f32[64,256]{1,0:T(8,128)} %param.14), channel_id=1, replica_groups=mesh['ia'=4,'ja'=2,'ka'=4] {'ka'}, dimensions={0}, use_global_device_ids=true | all-gather | bytes 327680 | tf_op jit(solution)/shard_map/all_gather | solution.py:35
  30.1 31.8 %all_gather.9 = f32[256,256]{1,0:T(8,128)S(1)} all-gather(f32[32,256]{1,0:T(8,128)} %param.13), channel_id=1, replica_groups=mesh['ia'=4,'ja'=2,'ka'=4] {'ja','ka'}, dimensions={0}, use_global_device_ids=true | all-gather | bytes 294912 | tf_op jit(solution)/shard_map/all_gather | solution.py:69
  62.0 34.4 %while.20 = (s32[]{:T(128)}, f32[256,256]{1,0:T(8,128)S(1)}, s32[4]{0:T(128)S(1)}, s32[4,64,4096]{2,1,0:T(8,128)}, bf16[256,256]{1,0:T(8,128)(2,1)S(1)}, /*index...) while((s32[]{:T(128)}, f32[256,256]{1,0:T(8,128)S(1)}, ...), condition=%wide.region_1.0_spmd, body=%wide.region_0.0_spmd.sunk | while | flops 271351808 | bytes 7899463 | solution.py:64
  63.3 0.7 dynamic_slice.109
  64.7 0.7 multiply_convert_fusion.4
  65.4 0.7 dynamic_slice.107
  66.8 0.7 dynamic_slice.110
  67.5 3.1 %fusion.52 = f32[256,256]{1,0:T(8,128)S(1)} fusion(f32[256,256]{1,0:T(8,128)S(1)} %get-tuple-element.345, s32[]{:T(128)S(6)} %select_n.33, bf16[4096,256]{1,0:T(8,128)(2,1)S(1)} %bitcast.70, s32[4,64,4096]{2,1,0:T(8,128)} %get-tuple-element.361, s32[]{:T(128)} %get-tuple-element.344, f32[]{:T(128)} %bitcast.60, ...), kind=kOutput, calls=%fused_computation.6.clone.1 | convolution fusion | flops 269254656 | bytes 5408768 | tf_op jit(solution)/shard_map/while/body/eval_jaxpr/dot_general | solution.py:26
  71.9 0.7 dynamic_slice.109
  73.3 0.7 multiply_convert_fusion.4
  74.0 0.7 dynamic_slice.107
  75.4 0.7 dynamic_slice.110
  76.1 3.1 %fusion.52 = f32[256,256]{1,0:T(8,128)S(1)} fusion(f32[256,256]{1,0:T(8,128)S(1)} %get-tuple-element.345, s32[]{:T(128)S(6)} %select_n.33, bf16[4096,256]{1,0:T(8,128)(2,1)S(1)} %bitcast.70, s32[4,64,4096]{2,1,0:T(8,128)} %get-tuple-element.361, s32[]{:T(128)} %get-tuple-element.344, f32[]{:T(128)} %bitcast.60, ...), kind=kOutput, calls=%fused_computation.6.clone.1 | convolution fusion | flops 269254656 | bytes 5408768 | tf_op jit(solution)/shard_map/while/body/eval_jaxpr/dot_general | solution.py:26
  80.5 0.7 dynamic_slice.109
  81.9 0.7 multiply_convert_fusion.4
  82.6 0.7 dynamic_slice.107
  84.0 0.7 dynamic_slice.110
  84.7 3.1 %fusion.52 = f32[256,256]{1,0:T(8,128)S(1)} fusion(f32[256,256]{1,0:T(8,128)S(1)} %get-tuple-element.345, s32[]{:T(128)S(6)} %select_n.33, bf16[4096,256]{1,0:T(8,128)(2,1)S(1)} %bitcast.70, s32[4,64,4096]{2,1,0:T(8,128)} %get-tuple-element.361, s32[]{:T(128)} %get-tuple-element.344, f32[]{:T(128)} %bitcast.60, ...), kind=kOutput, calls=%fused_computation.6.clone.1 | convolution fusion | flops 269254656 | bytes 5408768 | tf_op jit(solution)/shard_map/while/body/eval_jaxpr/dot_general | solution.py:26
  89.2 0.7 dynamic_slice.109
  90.5 0.7 multiply_convert_fusion.4
  92.6 0.7 dynamic_slice.110
  93.3 3.1 %fusion.52 = f32[256,256]{1,0:T(8,128)S(1)} fusion(f32[256,256]{1,0:T(8,128)S(1)} %get-tuple-element.345, s32[]{:T(128)S(6)} %select_n.33, bf16[4096,256]{1,0:T(8,128)(2,1)S(1)} %bitcast.70, s32[4,64,4096]{2,1,0:T(8,128)} %get-tuple-element.361, s32[]{:T(128)} %get-tuple-element.344, f32[]{:T(128)} %bitcast.60, ...), kind=kOutput, calls=%fused_computation.6.clone.1 | convolution fusion | flops 269254656 | bytes 5408768 | tf_op jit(solution)/shard_map/while/body/eval_jaxpr/dot_general | solution.py:26
  96.4 0.7 copy-done.1
  97.9 21.7 %psum.15 = f32[4,256]{1,0:T(4,128)S(1)} all-reduce(f32[4,256]{1,0:T(4,128)S(1)} %fusion.24), channel_id=1, replica_groups=mesh['ia'=4,'ja'=2,'ka'=4] {'ja','ka'}, use_global_device_ids=true, to_apply=%region_5.6 | all-reduce | flops 1024 | bytes 8192 | tf_op jit(solution)/shard_map/psum | solution.py:50
  119.5 49.9 %all-reduce.2.cloned.1.call-done = f32[256,256]{1,0:T(8,128)} async-done(((f32[256,256]{1,0:T(8,128)}), f32[256,256]{1,0:T(8,128)}) %all-reduce.2.cloned.1.call-update) | async-done | bytes 262160 | tf_op jit(solution)/shard_map/psum | solution.py:71
  169.4 1.0 fusion.33
  170.5 34.4 %while.21 = (s32[]{:T(128)}, f32[256,256]{1,0:T(8,128)S(1)}, s32[4]{0:T(128)S(1)}, s32[4,64,4096]{2,1,0:T(8,128)}, bf16[256,256]{1,0:T(8,128)(2,1)S(1)}, /*index...) while((s32[]{:T(128)}, f32[256,256]{1,0:T(8,128)S(1)}, ...), condition=%wide.region_7.8_spmd, body=%wide.region_6.7_spmd.sunk | while | flops 271351808 | bytes 7899463 | solution.py:64
  171.8 0.7 dynamic_slice.117
  173.2 0.7 multiply_convert_fusion.5
  173.9 0.7 dynamic_slice.115
  175.3 0.7 dynamic_slice.118
  176.0 3.1 %fusion.56 = f32[256,256]{1,0:T(8,128)S(1)} fusion(f32[256,256]{1,0:T(8,128)S(1)} %get-tuple-element.387, s32[]{:T(128)S(6)} %select_n.36, bf16[4096,256]{1,0:T(8,128)(2,1)S(1)} %bitcast.71, s32[4,64,4096]{2,1,0:T(8,128)} %get-tuple-element.403, s32[]{:T(128)} %get-tuple-element.386, f32[]{:T(128)} %bitcast.68, ...), kind=kOutput, calls=%fused_computation.20.clone.1 | convolution fusion | flops 269254656 | bytes 5408768 | tf_op jit(solution)/shard_map/while/body/eval_jaxpr/dot_general | solution.py:26
  180.4 0.7 dynamic_slice.117
  181.8 0.7 multiply_convert_fusion.5
  182.5 0.7 dynamic_slice.115
  183.9 0.7 dynamic_slice.118
  184.6 3.1 %fusion.56 = f32[256,256]{1,0:T(8,128)S(1)} fusion(f32[256,256]{1,0:T(8,128)S(1)} %get-tuple-element.387, s32[]{:T(128)S(6)} %select_n.36, bf16[4096,256]{1,0:T(8,128)(2,1)S(1)} %bitcast.71, s32[4,64,4096]{2,1,0:T(8,128)} %get-tuple-element.403, s32[]{:T(128)} %get-tuple-element.386, f32[]{:T(128)} %bitcast.68, ...), kind=kOutput, calls=%fused_computation.20.clone.1 | convolution fusion | flops 269254656 | bytes 5408768 | tf_op jit(solution)/shard_map/while/body/eval_jaxpr/dot_general | solution.py:26
  189.0 0.7 dynamic_slice.117
  190.4 0.7 multiply_convert_fusion.5
  191.1 0.7 dynamic_slice.115
  193.2 3.1 %fusion.56 = f32[256,256]{1,0:T(8,128)S(1)} fusion(f32[256,256]{1,0:T(8,128)S(1)} %get-tuple-element.387, s32[]{:T(128)S(6)} %select_n.36, bf16[4096,256]{1,0:T(8,128)(2,1)S(1)} %bitcast.71, s32[4,64,4096]{2,1,0:T(8,128)} %get-tuple-element.403, s32[]{:T(128)} %get-tuple-element.386, f32[]{:T(128)} %bitcast.68, ...), kind=kOutput, calls=%fused_computation.20.clone.1 | convolution fusion | flops 269254656 | bytes 5408768 | tf_op jit(solution)/shard_map/while/body/eval_jaxpr/dot_general | solution.py:26
  199.0 0.7 multiply_convert_fusion.5
  201.8 3.1 %fusion.56 = f32[256,256]{1,0:T(8,128)S(1)} fusion(f32[256,256]{1,0:T(8,128)S(1)} %get-tuple-element.387, s32[]{:T(128)S(6)} %select_n.36, bf16[4096,256]{1,0:T(8,128)(2,1)S(1)} %bitcast.71, s32[4,64,4096]{2,1,0:T(8,128)} %get-tuple-element.403, s32[]{:T(128)} %get-tuple-element.386, f32[]{:T(128)} %bitcast.68, ...), kind=kOutput, calls=%fused_computation.20.clone.1 | convolution fusion | flops 269254656 | bytes 5408768 | tf_op jit(solution)/shard_map/while/body/eval_jaxpr/dot_general | solution.py:26
  204.9 0.7 copy-done
  205.6 61.8 %reduce-scatter.2.cloned.1.call-done = f32[32,256]{1,0:T(8,128)} async-done(((f32[256,256]{1,0:T(8,128)}), f32[32,256]{1,0:T(8,128)}) %reduce-scatter.2.cloned.1.call-update) | async-done | bytes 32784 | tf_op jit(solution)/shard_map/reduce_scatter | solution.py:74
  267.4 1.4 dynamic-slice_divide_fusion
  (39 shorter events, 10.0 us)
Async XLA Ops:
  6.5 162.9 %all-reduce.2.cloned.1.call-start = ((), (), s32[]{:S(2)}) async-start(), calls=%async_computation.1 | async-start | bytes 524288 | tf_op jit(solution)/shard_map/psum | solution.py:71
  96.4 0.7 copy-start.1
  97.1 170.3 %reduce-scatter.2.cloned.1.call-start = ((), (), s32[]{:S(2)}) async-start(), calls=%async_computation.2 | async-start | bytes 294912 | tf_op jit(solution)/shard_map/reduce_scatter | solution.py:74
  204.9 0.7 copy-start
Sparse Core Ops, SparseCore 0:
  97.2 72.1 all-reduce.1
  205.7 61.6 reduce-scatter.1
where the time goes:
time: 277 us; the launch traced here: 276 us
  waiting for transfers between devices  112 us (40%)
  blocking collectives  75.3 us (27%)
  matrix products  25.4 us (9%)
  local copies, waits for them, and re-layouts  24 us (9%)
  loops' own time  17.1 us (6%)
  between operations  14.1 us (5%)
  other arithmetic  7.95 us (3%)
    reduce_scatter x1, waiting for transfers between devices, local(): mine = lax.psum_scatter(phi, ('ja', 'ka'), scatter_dimension=0, tiled=True)  61.8 us
    psum x1, waiting for transfers between devices, local(): totals = lax.psum(phi, ('ja', 'ka'))  49.9 us
    all_gather x1, blocking collectives, local(): whole = lax.all_gather(factor_a, ('ja', 'ka'), axis=0, tiled=True)  31.8 us
    dot_general x8, matrix products, add_block(): part = jnp.dot(ratio, panel, preferred_element_type=jnp.float32) * weight  24.7 us
    psum x1, blocking collectives, local(): mass = lax.psum(mass_part, ('ja', 'ka'))  21.7 us
    dynamic_slice x32, local copies, waits for them, and re-layouts, accumulate(): lax.scan(step, empty, (coords[:, 0], coords[:, 1], coords[:, 2], weights,...  21.4 us
    another operation x2, loops' own time, accumulate(): lax.scan(step, empty, (coords[:, 0], coords[:, 1], coords[:, 2], weights,...  17.1 us
    all_gather x1, blocking collectives, local(): rows_b = lax.all_gather(factor_b, 'ka', axis=0, tiled=True)  14.3 us
  transfers between devices with their start and end apart: 2, of which 2 were waited for; matrix products, arithmetic and copies ran while one was open for 0% of the time, Pallas kernels for 0%

commit v1 on v0

--- a/solution.py
+++ b/solution.py
@@ -68,7 +68,9 @@
 
     whole = lax.all_gather(factor_a, ("ja", "ka"), axis=0, tiled=True)
     phi = accumulate(whole.astype(jnp.bfloat16))
-    totals = lax.psum(phi, ("ja", "ka"))
+    totals = phi
+    for over in ("ja", "ka"):
+        totals = lax.psum(totals, over)
     updated = whole * totals / mass_rows
     phi = accumulate(updated.astype(jnp.bfloat16))
     mine = lax.psum_scatter(phi, ("ja", "ka"), scatter_dimension=0, tiled=True)

time: 277 us -> 267 us (0.964)
  waiting for transfers between devices: 112 us -> 104 us
    psum x1 -> x2, waiting for transfers between devices: 49.9 us -> 41.3 us  [local(): totals = lax.psum(totals, over)]
  transfers between devices with their start and end apart: 2 -> 3, of which waited for: 2 -> 3; matrix products, arithmetic and copies ran while one was open for 0% -> 0% of each run, Pallas kernels for 0% -> 0%
where the time goes in v1:
time: 267 us; the launch traced here: 266 us
  waiting for transfers between devices  104 us (39%)
  blocking collectives  74.2 us (28%)
  matrix products  25.4 us (10%)
  local copies, waits for them, and re-layouts  24 us (9%)
  loops' own time  17.1 us (6%)
  between operations  13.8 us (5%)
  other arithmetic  7.96 us (3%)
    reduce_scatter x1, waiting for transfers between devices, local(): mine = lax.psum_scatter(phi, ('ja', 'ka'), scatter_dimension=0, tiled=True)  62.4 us
    psum x2, waiting for transfers between devices, local(): totals = lax.psum(totals, over)  41.3 us
    all_gather x1, blocking collectives, local(): whole = lax.all_gather(factor_a, ('ja', 'ka'), axis=0, tiled=True)  31.8 us
    dot_general x8, matrix products, add_block(): part = jnp.dot(ratio, panel, preferred_element_type=jnp.float32) * weight  24.8 us
    dynamic_slice x32, local copies, waits for them, and re-layouts, accumulate(): lax.scan(step, empty, (coords[:, 0], coords[:, 1], coords[:, 2], weights,...  21.4 us
    psum x1, blocking collectives, local(): mass = lax.psum(mass_part, ('ja', 'ka'))  20.6 us
    another operation x2, loops' own time, accumulate(): lax.scan(step, empty, (coords[:, 0], coords[:, 1], coords[:, 2], weights,...  17.1 us
    all_gather x1, blocking collectives, local(): rows_b = lax.all_gather(factor_b, 'ka', axis=0, tiled=True)  14.3 us
  transfers between devices with their start and end apart: 3, of which 3 were waited for; matrix products, arithmetic and copies ran while one was open for 0% of the time, Pallas kernels for 0%

profile of v1, /device:TPU:0, one launch (start us, length us, event | category | flops | bytes accessed | tf_op | source)
XLA Modules:
  0.0 266.5 jit_solution(744197925904572931)
XLA Ops:
  6.5 0.8 copy.14
  7.5 7.5 %all_gather.11 = f32[256,256]{0,1:T(8,128)S(1)} all-gather(f32[256,64]{0,1:T(8,128)} %param.15), channel_id=1, replica_groups=mesh['ia'=4,'ja'=2,'ka'=4] {'ia'}, dimensions={1}, use_global_device_ids=true | all-gather | bytes 327680 | tf_op jit(solution)/shard_map/all_gather | solution.py:36
  15.1 14.3 %all_gather.10 = f32[256,256]{1,0:T(8,128)S(1)} all-gather(f32[64,256]{1,0:T(8,128)} %param.14), channel_id=1, replica_groups=mesh['ia'=4,'ja'=2,'ka'=4] {'ka'}, dimensions={0}, use_global_device_ids=true | all-gather | bytes 327680 | tf_op jit(solution)/shard_map/all_gather | solution.py:35
  30.1 31.8 %all_gather.9 = f32[256,256]{1,0:T(8,128)S(1)} all-gather(f32[32,256]{1,0:T(8,128)} %param.13), channel_id=1, replica_groups=mesh['ia'=4,'ja'=2,'ka'=4] {'ja','ka'}, dimensions={0}, use_global_device_ids=true | all-gather | bytes 294912 | tf_op jit(solution)/shard_map/all_gather | solution.py:69
  62.0 34.5 %while.20 = (s32[]{:T(128)}, f32[256,256]{1,0:T(8,128)S(1)}, s32[4]{0:T(128)S(1)}, s32[4,64,4096]{2,1,0:T(8,128)}, bf16[256,256]{1,0:T(8,128)(2,1)S(1)}, /*index...) while((s32[]{:T(128)}, f32[256,256]{1,0:T(8,128)S(1)}, ...), condition=%wide.region_1.0_spmd, body=%wide.region_0.0_spmd.sunk | while | flops 271351808 | bytes 7899463 | solution.py:64
  63.3 0.7 dynamic_slice.109
  64.7 0.7 multiply_convert_fusion.4
  65.4 0.7 dynamic_slice.107
  66.8 0.7 dynamic_slice.110
  67.5 3.1 %fusion.52 = f32[256,256]{1,0:T(8,128)S(1)} fusion(f32[256,256]{1,0:T(8,128)S(1)} %get-tuple-element.345, s32[]{:T(128)S(6)} %select_n.33, bf16[4096,256]{1,0:T(8,128)(2,1)S(1)} %bitcast.70, s32[4,64,4096]{2,1,0:T(8,128)} %get-tuple-element.361, s32[]{:T(128)} %get-tuple-element.344, f32[]{:T(128)} %bitcast.60, ...), kind=kOutput, calls=%fused_computation.6.clone.1 | convolution fusion | flops 269254656 | bytes 5408768 | tf_op jit(solution)/shard_map/while/body/eval_jaxpr/dot_general | solution.py:26
  71.9 0.7 dynamic_slice.109
  73.3 0.7 multiply_convert_fusion.4
  74.0 0.7 dynamic_slice.107
  75.4 0.7 dynamic_slice.110
  76.1 3.1 %fusion.52 = f32[256,256]{1,0:T(8,128)S(1)} fusion(f32[256,256]{1,0:T(8,128)S(1)} %get-tuple-element.345, s32[]{:T(128)S(6)} %select_n.33, bf16[4096,256]{1,0:T(8,128)(2,1)S(1)} %bitcast.70, s32[4,64,4096]{2,1,0:T(8,128)} %get-tuple-element.361, s32[]{:T(128)} %get-tuple-element.344, f32[]{:T(128)} %bitcast.60, ...), kind=kOutput, calls=%fused_computation.6.clone.1 | convolution fusion | flops 269254656 | bytes 5408768 | tf_op jit(solution)/shard_map/while/body/eval_jaxpr/dot_general | solution.py:26
  80.6 0.7 dynamic_slice.109
  82.0 0.7 multiply_convert_fusion.4
  82.6 0.7 dynamic_slice.107
  84.0 0.7 dynamic_slice.110
  84.7 3.1 %fusion.52 = f32[256,256]{1,0:T(8,128)S(1)} fusion(f32[256,256]{1,0:T(8,128)S(1)} %get-tuple-element.345, s32[]{:T(128)S(6)} %select_n.33, bf16[4096,256]{1,0:T(8,128)(2,1)S(1)} %bitcast.70, s32[4,64,4096]{2,1,0:T(8,128)} %get-tuple-element.361, s32[]{:T(128)} %get-tuple-element.344, f32[]{:T(128)} %bitcast.60, ...), kind=kOutput, calls=%fused_computation.6.clone.1 | convolution fusion | flops 269254656 | bytes 5408768 | tf_op jit(solution)/shard_map/while/body/eval_jaxpr/dot_general | solution.py:26
  89.2 0.7 dynamic_slice.109
  90.6 0.7 multiply_convert_fusion.4
  92.6 0.7 dynamic_slice.110
  93.3 3.1 %fusion.52 = f32[256,256]{1,0:T(8,128)S(1)} fusion(f32[256,256]{1,0:T(8,128)S(1)} %get-tuple-element.345, s32[]{:T(128)S(6)} %select_n.33, bf16[4096,256]{1,0:T(8,128)(2,1)S(1)} %bitcast.70, s32[4,64,4096]{2,1,0:T(8,128)} %get-tuple-element.361, s32[]{:T(128)} %get-tuple-element.344, f32[]{:T(128)} %bitcast.60, ...), kind=kOutput, calls=%fused_computation.6.clone.1 | convolution fusion | flops 269254656 | bytes 5408768 | tf_op jit(solution)/shard_map/while/body/eval_jaxpr/dot_general | solution.py:26
  96.4 0.7 copy-done.1
  97.4 24.3 %all-reduce.3.cloned.1.call-done = f32[256,256]{1,0:T(8,128)} async-done(((f32[256,256]{1,0:T(8,128)}), f32[256,256]{1,0:T(8,128)}) %all-reduce.3.cloned.1.call-update) | async-done | bytes 262160 | tf_op jit(solution)/shard_map/psum | solution.py:73
  122.2 20.6 %psum.23 = f32[4,256]{1,0:T(4,128)S(1)} all-reduce(f32[4,256]{1,0:T(4,128)S(1)} %fusion.24), channel_id=1, replica_groups=mesh['ia'=4,'ja'=2,'ka'=4] {'ja','ka'}, use_global_device_ids=true, to_apply=%region_6.7 | all-reduce | flops 1024 | bytes 8192 | tf_op jit(solution)/shard_map/psum | solution.py:50
  142.8 17.1 %all-reduce.5.cloned.1.call-done = f32[256,256]{1,0:T(8,128)} async-done(((f32[256,256]{1,0:T(8,128)}), f32[256,256]{1,0:T(8,128)}) %all-reduce.5.cloned.1.call-update) | async-done | bytes 262160 | tf_op jit(solution)/shard_map/psum | solution.py:73
  159.9 1.0 fusion.33
  160.9 34.4 %while.21 = (s32[]{:T(128)}, f32[256,256]{1,0:T(8,128)S(1)}, s32[4]{0:T(128)S(1)}, s32[4,64,4096]{2,1,0:T(8,128)}, bf16[256,256]{1,0:T(8,128)(2,1)S(1)}, /*index...) while((s32[]{:T(128)}, f32[256,256]{1,0:T(8,128)S(1)}, ...), condition=%wide.region_8.9_spmd, body=%wide.region_7.8_spmd.sunk | while | flops 271351808 | bytes 7899463 | solution.py:64
  162.3 0.7 dynamic_slice.117
  163.7 0.7 multiply_convert_fusion.5
  165.7 0.7 dynamic_slice.118
  166.4 3.1 %fusion.56 = f32[256,256]{1,0:T(8,128)S(1)} fusion(f32[256,256]{1,0:T(8,128)S(1)} %get-tuple-element.387, s32[]{:T(128)S(6)} %select_n.36, bf16[4096,256]{1,0:T(8,128)(2,1)S(1)} %bitcast.71, s32[4,64,4096]{2,1,0:T(8,128)} %get-tuple-element.403, s32[]{:T(128)} %get-tuple-element.386, f32[]{:T(128)} %bitcast.68, ...), kind=kOutput, calls=%fused_computation.20.clone.1 | convolution fusion | flops 269254656 | bytes 5408768 | tf_op jit(solution)/shard_map/while/body/eval_jaxpr/dot_general | solution.py:26
  170.9 0.7 dynamic_slice.117
  172.3 0.7 multiply_convert_fusion.5
  174.3 0.7 dynamic_slice.118
  175.0 3.1 %fusion.56 = f32[256,256]{1,0:T(8,128)S(1)} fusion(f32[256,256]{1,0:T(8,128)S(1)} %get-tuple-element.387, s32[]{:T(128)S(6)} %select_n.36, bf16[4096,256]{1,0:T(8,128)(2,1)S(1)} %bitcast.71, s32[4,64,4096]{2,1,0:T(8,128)} %get-tuple-element.403, s32[]{:T(128)} %get-tuple-element.386, f32[]{:T(128)} %bitcast.68, ...), kind=kOutput, calls=%fused_computation.20.clone.1 | convolution fusion | flops 269254656 | bytes 5408768 | tf_op jit(solution)/shard_map/while/body/eval_jaxpr/dot_general | solution.py:26
  179.5 0.7 dynamic_slice.117
  180.9 0.7 multiply_convert_fusion.5
  183.0 0.7 dynamic_slice.118
  183.6 3.1 %fusion.56 = f32[256,256]{1,0:T(8,128)S(1)} fusion(f32[256,256]{1,0:T(8,128)S(1)} %get-tuple-element.387, s32[]{:T(128)S(6)} %select_n.36, bf16[4096,256]{1,0:T(8,128)(2,1)S(1)} %bitcast.71, s32[4,64,4096]{2,1,0:T(8,128)} %get-tuple-element.403, s32[]{:T(128)} %get-tuple-element.386, f32[]{:T(128)} %bitcast.68, ...), kind=kOutput, calls=%fused_computation.20.clone.1 | convolution fusion | flops 269254656 | bytes 5408768 | tf_op jit(solution)/shard_map/while/body/eval_jaxpr/dot_general | solution.py:26
  188.1 0.7 dynamic_slice.117
  189.5 0.7 multiply_convert_fusion.5
  192.2 3.1 %fusion.56 = f32[256,256]{1,0:T(8,128)S(1)} fusion(f32[256,256]{1,0:T(8,128)S(1)} %get-tuple-element.387, s32[]{:T(128)S(6)} %select_n.36, bf16[4096,256]{1,0:T(8,128)(2,1)S(1)} %bitcast.71, s32[4,64,4096]{2,1,0:T(8,128)} %get-tuple-element.403, s32[]{:T(128)} %get-tuple-element.386, f32[]{:T(128)} %bitcast.68, ...), kind=kOutput, calls=%fused_computation.20.clone.1 | convolution fusion | flops 269254656 | bytes 5408768 | tf_op jit(solution)/shard_map/while/body/eval_jaxpr/dot_general | solution.py:26
  195.3 0.7 copy-done
  196.1 62.4 %reduce-scatter.2.cloned.1.call-done = f32[32,256]{1,0:T(8,128)} async-done(((f32[256,256]{1,0:T(8,128)}), f32[32,256]{1,0:T(8,128)}) %reduce-scatter.2.cloned.1.call-update) | async-done | bytes 32784 | tf_op jit(solution)/shard_map/reduce_scatter | solution.py:76
  258.5 1.4 dynamic-slice_divide_fusion
  (42 shorter events, 10.7 us)
Async XLA Ops:
  6.5 115.2 %all-reduce.3.cloned.1.call-start = ((), (), s32[]{:S(2)}) async-start(), calls=%async_computation.1 | async-start | bytes 524288 | tf_op jit(solution)/shard_map/psum | solution.py:73
  96.4 0.7 copy-start.1
  97.1 62.7 %all-reduce.5.cloned.1.call-start = ((), (), s32[]{:S(2)}) async-start(), calls=%async_computation.2 | async-start | bytes 524288 | tf_op jit(solution)/shard_map/psum | solution.py:73
  121.7 136.8 %reduce-scatter.2.cloned.1.call-start = ((), (), s32[]{:S(2)}) async-start(), calls=%async_computation.3 | async-start | bytes 294912 | tf_op jit(solution)/shard_map/reduce_scatter | solution.py:76
  195.3 0.7 copy-start
Sparse Core Ops, SparseCore 0:
  97.3 24.3 all-reduce.2
  124.0 35.7 all-reduce.4
  196.2 62.2 reduce-scatter.1
